TPU v7x, 32 devices: a whole 2x2x4 slice. The times are simulated.
32 devices in a mesh: space: 8 (over y, x, core), mode: 4 (over z).
Axes of the slice: x: 2, y: 2, z: 4, core: 2. Of those that a mesh axis runs over, the one named last changes fastest.
Arguments:
- start_modes: float32 [256, 24576], P('mode', 'space')
- hessian: bfloat16 [128, 8, 192, 192], P('space'), may hold values from -0.15625 to 0.15625
- block_exponent: int32 [128, 8], P('space'), may hold values from -1 to 1
- col_block: int32 [128, 8], P('space'), may hold values from 0 to 19, as said below
- grain_count: int32 [8], P('space'), may hold values from 384 to 512, as said below
Outputs:
- modes: float32 [256, 24576], P('mode', 'space')
Inputs may be any that keep to these rules, and one draw needn't show every extreme that they name: col_block[b, k] lies between b mod 16 and b mod 16 + 2 * 2; slot 0 is b mod 16 + 2; both ends are reached in every slab. `grain_count`: at most 512 grains a slab, reached by at least one slab.
All inputs are finite; a program needn't handle non-finite values.
Results may differ from a plain program's by a relative error of at most 0.0034.
Values may be sent and summed in bfloat16 or wider, within the bound.
A program may use at most 64 MiB of HBM per device.

v0:
```python
import jax
import jax.numpy as jnp
from jax import lax
from jax.sharding import PartitionSpec as P

HALO_BLOCKS = 2
filter_center = -0.5
filter_half = 1.5


def extended(cells, sides, width):
    for axis, dim in sides:
        count = lax.axis_size(axis)
        head = lax.slice_in_dim(cells, 0, width, axis=dim)
        tail = lax.slice_in_dim(cells, cells.shape[dim] - width, cells.shape[dim], axis=dim)
        cells = jnp.concatenate(
            [
                lax.ppermute(tail, axis, [(i, (i + 1) % count) for i in range(count)]),
                cells,
                lax.ppermute(head, axis, [((i + 1) % count, i) for i in range(count)]),
            ],
            axis=dim,
        )
    return cells


def per_device(start_modes, hessian, block_exponent, col_block, grain_count):
    panel_size, rows_here = start_modes.shape
    slab_blocks, contacts, block_size, _ = hessian.shape
    halo_width = HALO_BLOCKS * block_size
    places = lax.broadcasted_iota(jnp.int32, (rows_here,), 0)
    live = (places < 6 * grain_count[0]).astype(jnp.float32)
    scales = jnp.exp2(block_exponent.astype(jnp.float32)).astype(jnp.bfloat16)

    def operate(vectors_low):
        padded = extended(vectors_low, (("space", 1),), halo_width)
        window = padded.reshape(panel_size, slab_blocks + 2 * HALO_BLOCKS, block_size)
        gathered = jnp.take(window, col_block, axis=1)
        gathered = gathered * scales[None, :, :, None]
        image = jnp.einsum("rkij,prkj->pri", hessian, gathered, preferred_element_type=jnp.float32)
        return image.reshape(panel_size, rows_here)

    start = start_modes * live
    image = operate(start.astype(jnp.bfloat16))
    first = (image - filter_center * start) / filter_half * live
    image = operate(first.astype(jnp.bfloat16))
    second = (2.0 * (image - filter_center * first) / filter_half - start) * live
    my_index = lax.axis_index("mode")
    whole = lax.all_gather(second, "mode", axis=0, tiled=True)
    partial_rows = jnp.dot(
        second, whole.T, precision=lax.Precision.HIGHEST, preferred_element_type=jnp.float32
    )
    summed_rows = lax.psum(partial_rows, "space")
    gram = lax.all_gather(summed_rows, "mode", axis=0, tiled=True)
    lower_factor = jnp.linalg.cholesky(gram)
    identity_matrix = jnp.eye(gram.shape[0], dtype=jnp.float32)
    inverse_factor = jax.scipy.linalg.solve_triangular(lower_factor, identity_matrix, lower=True)
    own_inverse = lax.dynamic_slice_in_dim(inverse_factor, my_index * panel_size, panel_size, 0)
    return jnp.dot(
        own_inverse, whole, precision=lax.Precision.HIGHEST, preferred_element_type=jnp.float32
    )


def solution(mesh):
    return jax.shard_map(
        per_device,
        mesh=mesh,
        in_specs=(
            P("mode", "space"),
            P("space", None, None, None),
            P("space", None),
            P("space", None),
            P("space"),
        ),
        out_specs=P("mode", "space"),
        check_vma=False,
    )
```

profile of v0, /device:TPU:0, one launch (start us, length us, event | category | flops | bytes accessed | tf_op | source)
XLA Modules:
  0.0 278.4 jit_solution(5893356217424159986)
XLA Ops:
  9.0 2.9 %collective-permute-start.1 = (bf16[64,384]{1,0:T(8,128)(2,1)S(1)}, bf16[64,384]{1,0:T(8,128)(2,1)S(1)}, u32[]{:S(2)}, u32[]{:S(2)}) collective-permute-start(bf16[64,384]{1,0:T(8,128)(2,1)S(1)} %get-tuple-element.27), channel_id=1, source_target_pairs={{4,0},{8,4},{12,8},{16,12},{20,16},{24,20},{28,24},{0,28},{5,1},{9... | collective-permute-start | bytes 147464 | tf_op jit(solution)/shard_map/ppermute | solution.py:20
  15.3 2.8 gather_fusion
  18.1 11.0 %fusion.10 = f32[64,16,192]{2,0,1:T(8,128)} fusion(bf16[16,8,192,192]{3,2,1,0:T(8,128)(2,1)} %param.8, bf16[16,8,64,192]{3,2,1,0:T(8,128)(2,1)} %bitcast.60, pred[16,8]{1,0:T(8,128)(4,1)S(1)} %copy.26, bf16[16,8]{1,0:T(8,128)(2,1)S(1)} %copy.30), kind=kOutput, calls=%fused_computation.16 | convolution fusion | flops 607125504 | bytes 13369728 | tf_op jit(solution)/shard_map/rkij,prkj->pri/dot_general | solution.py:40
  29.1 1.9 copy.31
  32.3 1.9 collective-permute-start.3
  34.2 1.8 collective-permute-done.2
  36.8 1.9 reshape.46
  38.9 2.8 gather_fusion.1
  41.6 11.0 %fusion.11 = f32[64,16,192]{2,0,1:T(8,128)} fusion(bf16[16,8,192,192]{3,2,1,0:T(8,128)(2,1)} %param.8, bf16[16,8,64,192]{3,2,1,0:T(8,128)(2,1)} %bitcast.59, pred[16,8]{1,0:T(8,128)(4,1)S(1)} %copy.26, bf16[16,8]{1,0:T(8,128)(2,1)S(1)} %copy.30), kind=kOutput, calls=%fused_computation.17 | convolution fusion | flops 607125504 | bytes 13369728 | tf_op jit(solution)/shard_map/rkij,prkj->pri/dot_general | solution.py:40
  52.6 1.8 copy.34
  55.7 2.3 subtract_multiply_fusion
  58.2 65.6 %all-gather.2.cloned.1.call-done = f32[256,3072]{1,0:T(8,128)} async-done(((f32[64,3072]{1,0:T(8,128)}), f32[256,3072]{1,0:T(8,128)}) %all-gather.2.cloned.1.call-update) | async-done | bytes 3145744 | tf_op jit(solution)/shard_map/all_gather | solution.py:49
  123.8 5.9 %fusion.33 = f32[64,256]{1,0:T(8,128)} fusion(f32[64,3072]{1,0:T(8,128)} %subtract_multiply_fusion, f32[256,3072]{1,0:T(8,128)} %all-gather.2.cloned.1.call-done), kind=kOutput, calls=%fused_computation.68 | convolution fusion | flops 603979776 | bytes 3997696 | tf_op jit(solution)/shard_map/dot_general | solution.py:50
  129.7 52.0 %all-reduce.3.cloned.1.call-done = f32[64,256]{1,0:T(8,128)} async-done(((f32[64,256]{1,0:T(8,128)}), f32[64,256]{1,0:T(8,128)}) %all-reduce.3.cloned.1.call-update) | async-done | bytes 65552 | tf_op jit(solution)/shard_map/psum | solution.py:53
  181.7 14.1 %all_gather.7 = f32[256,256]{1,0:T(8,128)S(1)} all-gather(f32[64,256]{1,0:T(8,128)} %all-reduce.3.cloned.1.call-done), channel_id=1, replica_groups=mesh['space'=8,'mode'=4] {'mode'}, dimensions={0}, use_global_device_ids=true | all-gather | bytes 327680 | tf_op jit(solution)/shard_map/all_gather | solution.py:54
  198.4 11.7 %cholesky.50 = f32[128,128]{1,0:T(8,128)S(1)} custom-call(f32[128,128]{1,0:T(8,128)S(1)} %cholesky.118), custom_call_target="Cholesky" | custom-call | tf_op jit(solution)/shard_map/jit(cholesky)/cholesky | solution.py:55
  210.8 10.6 %custom-call.15 = f32[1,128,128]{1,2,0:T(8,128)S(1)} custom-call(f32[1,128,128]{2,1,0:T(8,128)} %get-tuple-element.31), custom_call_target="InvertDiagBlocksLowerTriangular" | custom-call | tf_op jit(solution)/shard_map/jit(cholesky)/cholesky | solution.py:55
  222.5 1.7 convolution_subtract_fusion.1
  224.2 12.5 %cholesky.105 = f32[128,128]{1,0:T(8,128)S(1)} custom-call(f32[128,128]{1,0:T(8,128)} %convolution_subtract_fusion.1), custom_call_target="Cholesky" | custom-call | tf_op jit(solution)/shard_map/jit(cholesky)/cholesky | solution.py:55
  239.8 5.2 %while.1 = (s32[]{:T(128)}, f32[256,256]{1,0:T(8,128)S(1)}, s32[2,2]{1,0:T(2,128)S(1)}, f32[2,128,128]{2,1,0:T(8,128)}, s32[]{:T(128)}) while((s32[]{:T(128)}, f32[256,256]{1,0:T(8,128)S(1)}, s32[2,2]{1,0:T(2,128)S(1)}, f32[2,128,128]{2,1,0:T(8,128)}, s32[]{:T(128)}) %tuple.26), condition=%wide.while_cond, body=%wide.while_body.sunk | while | flops 2 | bytes 132705 | solution.py:57
  240.6 1.9 bitcast_dynamic-update-slice_fusion.2
  243.1 1.9 bitcast_dynamic-update-slice_fusion.2
  245.0 21.1 %custom-call.16 = f32[2,128,128]{1,2,0:T(8,128)} custom-call(f32[2,128,128]{2,1,0:T(8,128)} %get-tuple-element.13), custom_call_target="InvertDiagBlocksLowerTriangular" | custom-call | tf_op jit(solution)/shard_map/jit(_solve_triangular)/triangular_solve | solution.py:57
  268.7 2.9 %fusion.17 = f32[64,3072]{1,0:T(8,128)} fusion(f32[256,3072]{1,0:T(8,128)S(1)} %copy-done, s32[]{:T(128)S(6)} %select_n.15, f32[128,256]{1,0:T(8,128)S(1)} %fusion.14, f32[128,256]{1,0:T(8,128)S(1)} %fusion.20), kind=kOutput, calls=%fused_computation.36 | convolution fusion | flops 603996160 | bytes 4194308 | tf_op jit(solution)/shard_map/dot_general | solution.py:59
  (58 shorter events, 18.7 us)
Async XLA Ops:
  6.5 117.3 %all-gather.2.cloned.1.call-start = ((), (), s32[]{:S(2)}) async-start(), calls=%async_computation | async-start | bytes 3932160 | tf_op jit(solution)/shard_map/all_gather | solution.py:49
  8.4 5.9 %collective-permute-start = (bf16[64,384]{1,0:T(8,128)(2,1)S(1)}, bf16[64,384]{1,0:T(8,128)(2,1)S(1)}, u32[]{:S(2)}, u32[]{:S(2)}) collective-permute-start(bf16[64,384]{1,0:T(8,128)(2,1)S(1)} %get-tuple-element.26), channel_id=1, source_target_pairs={{0,4},{4,8},{8,12},{12,16},{16,20},{20,24},{24,28},{28,0},{1,5},{5... | collective-permute-start | bytes 147464 | tf_op jit(solution)/shard_map/ppermute | solution.py:18
  9.0 5.4 %collective-permute-start.1 = (bf16[64,384]{1,0:T(8,128)(2,1)S(1)}, bf16[64,384]{1,0:T(8,128)(2,1)S(1)}, u32[]{:S(2)}, u32[]{:S(2)}) collective-permute-start(bf16[64,384]{1,0:T(8,128)(2,1)S(1)} %get-tuple-element.27), channel_id=1, source_target_pairs={{4,0},{8,4},{12,8},{16,12},{20,16},{24,20},{28,24},{0,28},{5,1},{9... | collective-permute-start | bytes 147464 | tf_op jit(solution)/shard_map/ppermute | solution.py:20
  29.1 2.3 copy-start.1
  31.5 4.5 %collective-permute-start.2 = (bf16[64,384]{1,0:T(8,128)(2,1)S(1)}, bf16[64,384]{1,0:T(8,128)(2,1)S(1)}, u32[]{:S(2)}, u32[]{:S(2)}) collective-permute-start(bf16[64,384]{1,0:T(8,128)(2,1)S(1)} %get-tuple-element.24), channel_id=1, source_target_pairs={{0,4},{4,8},{8,12},{12,16},{16,20},{20,24},{24,28},{28,0},{1,5},{5... | collective-permute-start | bytes 147464 | tf_op jit(solution)/shard_map/ppermute | solution.py:18
  32.3 3.7 %collective-permute-start.3 = (bf16[64,384]{1,0:T(8,128)(2,1)S(1)}, bf16[64,384]{1,0:T(8,128)(2,1)S(1)}, u32[]{:S(2)}, u32[]{:S(2)}) collective-permute-start(bf16[64,384]{1,0:T(8,128)(2,1)S(1)} %get-tuple-element.25), channel_id=1, source_target_pairs={{4,0},{8,4},{12,8},{16,12},{20,16},{24,20},{28,24},{0,28},{5,1},{9... | collective-permute-start | bytes 147464 | tf_op jit(solution)/shard_map/ppermute | solution.py:20
  58.0 123.8 %all-reduce.3.cloned.1.call-start = ((), (), s32[]{:S(2)}) async-start(), calls=%async_computation.1 | async-start | bytes 131072 | tf_op jit(solution)/shard_map/psum | solution.py:53
  123.8 144.9 %copy-start = (f32[256,3072]{1,0:T(8,128)S(1)}, f32[256,3072]{1,0:T(8,128)}, u32[]{:S(2)}) copy-start(f32[256,3072]{1,0:T(8,128)} %all-gather.2.cloned.1.call-done) | copy-start | bytes 9437188
  197.7 0.7 copy-start.3
  236.8 2.0 copy-start.2
Sparse Core Ops, SparseCore 0:
  58.1 65.6 all-gather.1
  129.8 51.8 all-reduce.2
where the time goes:
time: 279 us; the launch traced here: 278 us
  waiting for transfers between devices  119 us (43%)
  other arithmetic  65.9 us (24%)
  matrix products  36 us (13%)
  local copies, waits for them, and re-layouts  20.9 us (7%)
  between operations  15.5 us (6%)
  blocking collectives  14.1 us (5%)
  starting transfers between devices  6.4 us (2%)
    all_gather x1, waiting for transfers between devices, per_device(): whole = lax.all_gather(second, 'mode', axis=0, tiled=True)  65.6 us
    psum x1, waiting for transfers between devices, per_device(): summed_rows = lax.psum(partial_rows, 'space')  52 us
    another operation x6, other arithmetic, per_device(): lower_factor = jnp.linalg.cholesky(gram)  36.3 us
    another operation x3, other arithmetic, per_device(): jax.scipy.linalg.solve_triangular(lower_factor, identity_matrix, lower=True)  22.1 us
    dot_general x2, matrix products, operate(): jnp.einsum('rkij,prkj->pri', hessian, gathered, preferred_element_type=jn...  22 us
    all_gather x1, blocking collectives, per_device(): gram = lax.all_gather(summed_rows, 'mode', axis=0, tiled=True)  14.1 us
    dot_general x1, matrix products, per_device(): jnp.dot(second, whole.T, precision=lax.Precision.HIGHEST, preferred_eleme...  5.88 us
  transfers between devices with their start and end apart: 6, of which 3 were waited for; matrix products, arithmetic and copies ran while one was open for 1% of the time, Pallas kernels for 0%

commit v1 on v0

--- a/solution.py
+++ b/solution.py
@@ -6,6 +6,16 @@
 HALO_BLOCKS = 2
 filter_center = -0.5
 filter_half = 1.5
+
+
+def around_the_ring(x, axis, d):
+    size = lax.axis_size(axis)
+    held, pieces = (x, [x])
+    for _ in range(size - 1):
+        held = lax.ppermute(held, axis, [(i, (i + 1) % size) for i in range(size)])
+        pieces.insert(0, held)
+    line = jnp.concatenate(pieces, axis=d)
+    return jnp.roll(line, (lax.axis_index(axis) + 1) * x.shape[d], axis=d)
 
 
 def extended(cells, sides, width):
@@ -46,7 +56,7 @@
     image = operate(first.astype(jnp.bfloat16))
     second = (2.0 * (image - filter_center * first) / filter_half - start) * live
     my_index = lax.axis_index("mode")
-    whole = lax.all_gather(second, "mode", axis=0, tiled=True)
+    whole = around_the_ring(second, "mode", 0)
     partial_rows = jnp.dot(
         second, whole.T, precision=lax.Precision.HIGHEST, preferred_element_type=jnp.float32
     )

time: 279 us -> 263 us (0.943)
  other arithmetic: 65.9 us -> 58.6 us
  waiting for transfers between devices: 119 us -> 114 us
  matrix products: 36 us -> 31.7 us
    all_gather x1 -> x0, waiting for transfers between devices: 65.6 us -> none  [per_device(): whole = lax.all_gather(second, 'mode', axis=0, tiled=True)]
    ppermute x0 -> x3, waiting for transfers between devices: none -> 61.4 us  [around_the_ring(): held = lax.ppermute(held, axis, [(i, (i + 1) % size) for i in range(size)])]
  transfers between devices with their start and end apart: 6 -> 8, of which waited for: 3 -> 5; matrix products, arithmetic and copies ran while one was open for 1% -> 1% of each run, Pallas kernels for 0% -> 0%
where the time goes in v1:
time: 263 us
  waiting for transfers between devices  114 us (43%)
  other arithmetic  58.6 us (22%)
  matrix products  31.7 us (12%)
  local copies, waits for them, and re-layouts  20.2 us (8%)
  between operations  15.6 us (6%)
  blocking collectives  14.1 us (5%)
  starting transfers between devices  8.51 us (3%)
    ppermute x3, waiting for transfers between devices, around_the_ring(): held = lax.ppermute(held, axis, [(i, (i + 1) % size) for i in range(size)])  61.4 us
    psum x1, waiting for transfers between devices, per_device(): summed_rows = lax.psum(partial_rows, 'space')  50.7 us
    another operation x6, other arithmetic, per_device(): lower_factor = jnp.linalg.cholesky(gram)  34 us
    dot_general x2, matrix products, operate(): jnp.einsum('rkij,prkj->pri', hessian, gathered, preferred_element_type=jn...  22 us
    another operation x3, other arithmetic, per_device(): jax.scipy.linalg.solve_triangular(lower_factor, identity_matrix, lower=True)  19.7 us
    all_gather x1, blocking collectives, per_device(): gram = lax.all_gather(summed_rows, 'mode', axis=0, tiled=True)  14.1 us
    gather x2, local copies, waits for them, and re-layouts, operate(): gathered = jnp.take(window, col_block, axis=1)  5.49 us
  transfers between devices with their start and end apart: 8, of which 5 were waited for; matrix products, arithmetic and copies ran while one was open for 1% of the time, Pallas kernels for 0%

profile of v1, /device:TPU:0, one launch (start us, length us, event | category | flops | bytes accessed | tf_op | source)
XLA Modules:
  0.0 263.0 jit_solution(2030854101296056298)
XLA Ops:
  9.0 2.9 %collective-permute-start.1 = (bf16[64,384]{1,0:T(8,128)(2,1)S(1)}, bf16[64,384]{1,0:T(8,128)(2,1)S(1)}, u32[]{:S(2)}, u32[]{:S(2)}) collective-permute-start(bf16[64,384]{1,0:T(8,128)(2,1)S(1)} %get-tuple-element.27), channel_id=1, source_target_pairs={{4,0},{8,4},{12,8},{16,12},{20,16},{24,20},{28,24},{0,28},{5,1},{9... | collective-permute-start | bytes 147464 | tf_op jit(solution)/shard_map/ppermute | solution.py:30
  15.3 2.7 %gather_fusion = bf16[128,64,192]{2,1,0:T(8,128)(2,1)} fusion(bf16[64,20,192]{2,0,1:T(8,128)(2,1)S(1)} %copy.29, s32[1024]{0:T(1024)S(1)} %pad_clamp_fusion), kind=kCustom, calls=%fused_computation.clone | custom fusion | bytes 6291968 | tf_op jit(solution)/shard_map/jit(_take)/gather | solution.py:48
  18.1 11.0 %fusion.14 = f32[64,16,192]{2,0,1:T(8,128)} fusion(bf16[16,8,192,192]{3,2,1,0:T(8,128)(2,1)} %param.8, bf16[16,8,64,192]{3,2,1,0:T(8,128)(2,1)} %bitcast.58, pred[16,8]{1,0:T(8,128)(4,1)S(1)} %copy.26, bf16[16,8]{1,0:T(8,128)(2,1)S(1)} %copy.30), kind=kOutput, calls=%fused_computation.20 | convolution fusion | flops 607125504 | bytes 13369728 | tf_op jit(solution)/shard_map/rkij,prkj->pri/dot_general | solution.py:50
  29.1 1.8 copy.31
  32.3 1.9 collective-permute-start.3
  34.2 1.8 collective-permute-done.2
  37.0 2.7 %gather_fusion.1 = bf16[128,64,192]{2,1,0:T(8,128)(2,1)} fusion(bf16[64,20,192]{2,0,1:T(8,128)(2,1)S(1)} %copy.33, s32[1024]{0:T(1024)S(1)} %pad_clamp_fusion), kind=kCustom, calls=%fused_computation.1.clone | custom fusion | bytes 6291968 | tf_op jit(solution)/shard_map/jit(_take)/gather | solution.py:48
  39.7 11.0 %fusion.15 = f32[64,16,192]{2,0,1:T(8,128)} fusion(bf16[16,8,192,192]{3,2,1,0:T(8,128)(2,1)} %param.8, bf16[16,8,64,192]{3,2,1,0:T(8,128)(2,1)} %bitcast.57, pred[16,8]{1,0:T(8,128)(4,1)S(1)} %copy.26, bf16[16,8]{1,0:T(8,128)(2,1)S(1)} %copy.30), kind=kOutput, calls=%fused_computation.21 | convolution fusion | flops 607125504 | bytes 13369728 | tf_op jit(solution)/shard_map/rkij,prkj->pri/dot_general | solution.py:50
  50.7 1.8 copy.34
  53.8 1.4 subtract_multiply_fusion
  55.2 2.3 collective-permute-start.4
  57.5 20.1 %collective-permute-done.4 = f32[64,3072]{1,0:T(8,128)S(1)} collective-permute-done((f32[64,3072]{1,0:T(8,128)S(1)}, f32[64,3072]{1,0:T(8,128)S(1)}, u32[]{:S(2)}, u32[]{:S(2)}) %collective-permute-start.4) | collective-permute-done | bytes 786464 | tf_op jit(solution)/shard_map/ppermute | solution.py:15
  77.6 21.1 %collective-permute-done.5 = f32[64,3072]{1,0:T(8,128)S(1)} collective-permute-done((f32[64,3072]{1,0:T(8,128)S(1)}, f32[64,3072]{1,0:T(8,128)S(1)}, u32[]{:S(2)}, u32[]{:S(2)}) %collective-permute-start.5) | collective-permute-done | bytes 786464 | tf_op jit(solution)/shard_map/ppermute | solution.py:15
  98.7 20.2 %collective-permute-done.6 = f32[64,3072]{1,0:T(8,128)S(1)} collective-permute-done((f32[64,3072]{1,0:T(8,128)S(1)}, f32[64,3072]{1,0:T(8,128)S(1)}, u32[]{:S(2)}, u32[]{:S(2)}) %collective-permute-start.6) | collective-permute-done | bytes 786464 | tf_op jit(solution)/shard_map/ppermute | solution.py:15
  119.4 2.6 %copy-done = f32[512,3072]{1,0:T(8,128)} copy-done((f32[512,3072]{1,0:T(8,128)}, f32[512,3072]{1,0:T(8,128)S(1)}, u32[]{:S(2)}) %copy-start) | copy-done | bytes 6291480
  122.1 3.6 %fusion.8 = f32[64,256]{1,0:T(8,128)} fusion(f32[64,3072]{1,0:T(8,128)S(1)} %subtract_multiply_fusion, f32[512,3072]{1,0:T(8,128)S(1)} %constant_dynamic-update-slice_fusion, s32[]{:T(128)S(6)} %select_n.28), kind=kOutput, calls=%fused_computation.14 | convolution fusion | flops 603979776 | bytes 3997700 | tf_op jit(solution)/shard_map/dot_general | solution.py:60
  125.7 50.7 %all-reduce.3.cloned.1.call-done = f32[64,256]{1,0:T(8,128)} async-done(((f32[64,256]{1,0:T(8,128)}), f32[64,256]{1,0:T(8,128)}) %all-reduce.3.cloned.1.call-update) | async-done | bytes 65552 | tf_op jit(solution)/shard_map/psum | solution.py:63
  176.5 14.1 %all_gather.3 = f32[256,256]{1,0:T(8,128)S(1)} all-gather(f32[64,256]{1,0:T(8,128)} %all-reduce.3.cloned.1.call-done), channel_id=1, replica_groups=mesh['space'=8,'mode'=4] {'mode'}, dimensions={0}, use_global_device_ids=true | all-gather | bytes 327680 | tf_op jit(solution)/shard_map/all_gather | solution.py:64
  190.8 11.7 %cholesky.50 = f32[128,128]{1,0:T(8,128)S(1)} custom-call(f32[128,128]{1,0:T(8,128)S(1)} %cholesky.118), custom_call_target="Cholesky" | custom-call | tf_op jit(solution)/shard_map/jit(cholesky)/cholesky | solution.py:65
  202.6 9.8 %custom-call.15 = f32[1,128,128]{1,2,0:T(8,128)S(1)} custom-call(f32[1,128,128]{2,1,0:T(8,128)S(1)} %get-tuple-element.31), custom_call_target="InvertDiagBlocksLowerTriangular" | custom-call | tf_op jit(solution)/shard_map/jit(cholesky)/cholesky | solution.py:65
  212.9 11.7 %cholesky.105 = f32[128,128]{1,0:T(8,128)S(1)} custom-call(f32[128,128]{1,0:T(8,128)S(1)} %convolution_subtract_fusion.1), custom_call_target="Cholesky" | custom-call | tf_op jit(solution)/shard_map/jit(cholesky)/cholesky | solution.py:65
  226.7 4.1 %while.1 = (s32[]{:T(128)}, f32[256,256]{1,0:T(8,128)S(1)}, s32[2,2]{1,0:T(2,128)S(1)}, f32[2,128,128]{2,1,0:T(8,128)S(1)}, s32[]{:T(128)}) while((s32[]{:T(128)}, f32[256,256]{1,0:T(8,128)S(1)}, s32[2,2]{1,0:T(2,128)S(1)}, f32[2,128,128]{2,1,0:T(8,128)S(1)}, s32[]{:T(128)}) %tuple.26), condition=%wide.while_cond, body=%wide.while_body.sunk | while | flops 2 | bytes 131181 | solution.py:67
  230.8 19.7 %custom-call.16 = f32[2,128,128]{1,2,0:T(8,128)S(1)} custom-call(f32[2,128,128]{2,1,0:T(8,128)S(1)} %get-tuple-element.13), custom_call_target="InvertDiagBlocksLowerTriangular" | custom-call | tf_op jit(solution)/shard_map/jit(_solve_triangular)/triangular_solve | solution.py:67
  251.4 4.8 %fusion.6 = f32[64,3072]{1,0:T(8,128)} fusion(f32[512,3072]{1,0:T(8,128)} %copy-done, s32[]{:T(128)S(6)} %select_n.28, s32[]{:T(128)S(6)} %select_n.30, f32[128,256]{1,0:T(8,128)S(1)} %fusion.18, f32[128,256]{1,0:T(8,128)S(1)} %fusion.23), kind=kOutput, calls=%fused_computation.12 | convolution fusion | flops 603996160 | bytes 4194312 | tf_op jit(solution)/shard_map/dot_general | solution.py:69
  (65 shorter events, 15.5 us)
Async XLA Ops:
  6.5 169.9 %all-reduce.3.cloned.1.call-start = ((), (), s32[]{:S(2)}) async-start(), calls=%async_computation | async-start | bytes 131072 | tf_op jit(solution)/shard_map/psum | solution.py:63
  8.4 5.9 %collective-permute-start = (bf16[64,384]{1,0:T(8,128)(2,1)S(1)}, bf16[64,384]{1,0:T(8,128)(2,1)S(1)}, u32[]{:S(2)}, u32[]{:S(2)}) collective-permute-start(bf16[64,384]{1,0:T(8,128)(2,1)S(1)} %get-tuple-element.26), channel_id=1, source_target_pairs={{0,4},{4,8},{8,12},{12,16},{16,20},{20,24},{24,28},{28,0},{1,5},{5... | collective-permute-start | bytes 147464 | tf_op jit(solution)/shard_map/ppermute | solution.py:28
  9.0 5.4 %collective-permute-start.1 = (bf16[64,384]{1,0:T(8,128)(2,1)S(1)}, bf16[64,384]{1,0:T(8,128)(2,1)S(1)}, u32[]{:S(2)}, u32[]{:S(2)}) collective-permute-start(bf16[64,384]{1,0:T(8,128)(2,1)S(1)} %get-tuple-element.27), channel_id=1, source_target_pairs={{4,0},{8,4},{12,8},{16,12},{20,16},{24,20},{28,24},{0,28},{5,1},{9... | collective-permute-start | bytes 147464 | tf_op jit(solution)/shard_map/ppermute | solution.py:30
  18.1 13.3 %copy-start.1 = (f32[64,3072]{1,0:T(8,128)S(1)}, f32[64,3072]{1,0:T(8,128)}, u32[]{:S(2)}) copy-start(f32[64,3072]{1,0:T(8,128)} %param.7) | copy-start | bytes 2359300
  31.5 4.5 %collective-permute-start.2 = (bf16[64,384]{1,0:T(8,128)(2,1)S(1)}, bf16[64,384]{1,0:T(8,128)(2,1)S(1)}, u32[]{:S(2)}, u32[]{:S(2)}) collective-permute-start(bf16[64,384]{1,0:T(8,128)(2,1)S(1)} %get-tuple-element.24), channel_id=1, source_target_pairs={{0,4},{4,8},{8,12},{12,16},{16,20},{20,24},{24,28},{28,0},{1,5},{5... | collective-permute-start | bytes 147464 | tf_op jit(solution)/shard_map/ppermute | solution.py:28
  32.3 3.7 %collective-permute-start.3 = (bf16[64,384]{1,0:T(8,128)(2,1)S(1)}, bf16[64,384]{1,0:T(8,128)(2,1)S(1)}, u32[]{:S(2)}, u32[]{:S(2)}) collective-permute-start(bf16[64,384]{1,0:T(8,128)(2,1)S(1)} %get-tuple-element.25), channel_id=1, source_target_pairs={{4,0},{8,4},{12,8},{16,12},{20,16},{24,20},{28,24},{0,28},{5,1},{9... | collective-permute-start | bytes 147464 | tf_op jit(solution)/shard_map/ppermute | solution.py:30
  55.2 22.5 %collective-permute-start.4 = (f32[64,3072]{1,0:T(8,128)S(1)}, f32[64,3072]{1,0:T(8,128)S(1)}, u32[]{:S(2)}, u32[]{:S(2)}) collective-permute-start(f32[64,3072]{1,0:T(8,128)S(1)} %subtract_multiply_fusion), channel_id=1, source_target_pairs={{0,1},{1,2},{2,3},{3,0},{4,5},{5,6},{6,7},{7,4},{8,9},{9,10},{10,1... | collective-permute-start | bytes 2359304 | tf_op jit(solution)/shard_map/ppermute | solution.py:15
  77.6 21.1 %collective-permute-start.5 = (f32[64,3072]{1,0:T(8,128)S(1)}, f32[64,3072]{1,0:T(8,128)S(1)}, u32[]{:S(2)}, u32[]{:S(2)}) collective-permute-start(f32[64,3072]{1,0:T(8,128)S(1)} %collective-permute-done.4), channel_id=1, source_target_pairs={{0,1},{1,2},{2,3},{3,0},{4,5},{5,6},{6,7},{7,4},{8,9},{9,10},{10,1... | collective-permute-start | bytes 2359304 | tf_op jit(solution)/shard_map/ppermute | solution.py:15
  98.7 20.2 %collective-permute-start.6 = (f32[64,3072]{1,0:T(8,128)S(1)}, f32[64,3072]{1,0:T(8,128)S(1)}, u32[]{:S(2)}, u32[]{:S(2)}) collective-permute-start(f32[64,3072]{1,0:T(8,128)S(1)} %collective-permute-done.5), channel_id=1, source_target_pairs={{0,1},{1,2},{2,3},{3,0},{4,5},{5,6},{6,7},{7,4},{8,9},{9,10},{10,1... | collective-permute-start | bytes 2359304 | tf_op jit(solution)/shard_map/ppermute | solution.py:15
  119.4 2.6 %copy-start = (f32[512,3072]{1,0:T(8,128)}, f32[512,3072]{1,0:T(8,128)S(1)}, u32[]{:S(2)}) copy-start(f32[512,3072]{1,0:T(8,128)S(1)} %constant_dynamic-update-slice_fusion) | copy-start | bytes 18874372
Sparse Core Ops, SparseCore 0:
  125.8 50.5 all-reduce.2
